TPU v7x, 256 devices: a whole 4x4x8 slice. The times are simulated.
256 devices in a mesh: lev: 8 (over z_lo, x), hor: 32 (over z_hi, y, core).
Axes of the slice: x: 4, y: 4, z: 8 (z_hi: 4, z_lo: 2; z = z_hi * 2 + z_lo), core: 2. Of those that a mesh axis runs over, the one named last changes fastest.
Arguments:
- slab_fields: float32 [4, 32, 524288], P(None, 'lev', 'hor'), may hold values from -6 to 6
- sample_index: int32 [32, 1024], P('hor', 'lev'), may hold values from 0 to 2047
- thickness: float32 [32], replicated, may hold values from 0.3 to 3
- level_cuts: int32 [31], replicated, may hold values 0 or 1
Outputs:
- gram: float32 [2176, 2176], P('hor', 'lev')
Inputs may be any that keep to these rules, and one draw needn't show every extreme that they name: sample_index[j, k] indexes a column among the 2048 columns that start at j * 16384 + (k // 128) * 2048.
All inputs are finite; a program needn't handle non-finite values.
Results may differ from a plain program's by a relative error of at most 0.00068.
Values may be sent and summed in bfloat16 or wider, within the bound.
No kernel may reach another device: no remote copies, remote signals or barrier semaphores. Data moves between devices by JAX's collectives and lax.ppermute only.
A program may use at most 128 MiB of HBM per device.

v0:
```python
import jax
import jax.numpy as jnp
from jax import lax
from jax.sharding import PartitionSpec as P


def vertical_filter(values, thickness, level_cuts):
    link = 1.0 - level_cuts.astype(jnp.float32)
    zero_one = jnp.zeros((1,), jnp.float32)
    lower_link = jnp.concatenate([zero_one, link])
    upper_link = jnp.concatenate([link, zero_one])
    lower_weight = jnp.concatenate([zero_one, thickness[:-1]]) * lower_link
    upper_weight = jnp.concatenate([thickness[1:], zero_one]) * upper_link
    zero_row = jnp.zeros_like(values[:, :1, :])
    below = jnp.concatenate([zero_row, values[:, :-1, :]], axis=1)
    above = jnp.concatenate([values[:, 1:, :], zero_row], axis=1)
    numer = (
        2.0 * thickness[None, :, None] * values
        + lower_weight[None, :, None] * below
        + upper_weight[None, :, None] * above
    )
    denom = 2.0 * thickness + lower_weight + upper_weight
    return numer / denom[None, :, None]


def quadratic_features(smooth):
    count = smooth.shape[2]
    later = jnp.concatenate([smooth[2], smooth[3]], axis=0)
    earlier = jnp.concatenate([smooth[0], smooth[1]], axis=0)
    product = (later[:, None, :] * smooth[0][None, :, :]).reshape(-1, count)
    return jnp.concatenate([later, earlier, product], axis=0).astype(jnp.bfloat16)


def on_device(slab_fields, sample_index, thickness, level_cuts):
    samp_count = sample_index.shape[1]
    lev_count = lax.axis_size("lev")
    hor_count = lax.axis_size("hor")
    all_lists = lax.all_gather(sample_index, "lev", axis=1, tiled=True)[0]
    group_cols = slab_fields.shape[2] // lev_count
    offsets = jnp.arange(all_lists.shape[0]) // samp_count * group_cols + all_lists
    chosen = jnp.take(slab_fields, offsets, axis=2)
    picked_cols = lax.all_to_all(chosen, "lev", split_axis=2, concat_axis=1, tiled=True)
    smooth = vertical_filter(picked_cols, thickness, level_cuts)
    feat_count = 4 * smooth.shape[1] + 2 * smooth.shape[1] * smooth.shape[1]
    col_count = feat_count // lev_count
    col_start = lax.axis_index("lev") * col_count
    features_bf = quadratic_features(smooth)
    block_features_bf = lax.all_gather(features_bf, "lev", axis=1, tiled=True)
    chosen_rows = lax.dynamic_slice_in_dim(block_features_bf, col_start, col_count, 0)
    column_block = lax.dot_general(
        block_features_bf, chosen_rows, (((1,), (1,)), ((), ())), preferred_element_type=jnp.float32
    )
    gram_block = lax.psum_scatter(column_block, "hor", scatter_dimension=0, tiled=True)
    count_all = samp_count * lev_count * hor_count
    return gram_block / count_all


def solution(mesh):
    in_specs = (P(None, "lev", "hor"), P("hor", "lev"), P(), P())
    out_specs = P("hor", "lev")
    return jax.shard_map(
        on_device, mesh=mesh, in_specs=in_specs, out_specs=out_specs, check_vma=False
    )
```

profile of v0, /device:TPU:26, one launch (start us, length us, event | category | flops | bytes accessed | tf_op | source)
XLA Modules:
  0.0 281.2 jit_solution(17869697223792710759)
XLA Ops:
  6.5 0.0 copy-start.2
  6.5 21.7 %copy.7 = f32[4,4,16384]{1,0,2:T(4,128)} copy(f32[4,4,16384]{2,1,0:T(4,128)} %param.4) | data formatting | bytes 2097152 | tf_op args[0]
  28.2 0.0 copy-done.2
  28.2 0.0 copy-start.1
  28.2 0.0 copy-start.3
  28.3 16.4 %all_gather.6 = s32[1,1024]{1,0:T(1,128)S(1)} all-gather(s32[1,128]{1,0:T(1,128)S(1)} %copy-done.2), channel_id=1, replica_groups=mesh['lev'=8,'hor'=32] {'lev'}, dimensions={1}, use_global_device_ids=true | all-gather | bytes 4608 | tf_op jit(solution)/shard_map/all_gather | solution.py:38
  44.7 16.8 %gather_fusion = f32[1024,4,4]{2,1,0:T(4,128)} fusion(f32[4,4,16384]{1,0,2:T(4,128)} %copy.7, s32[1024]{0:T(1024)S(1)} %broadcast_clamp_fusion), kind=kCustom, calls=%fused_computation | custom fusion | bytes 135168 | tf_op jit(solution)/shard_map/jit(_take)/gather | solution.py:41
  61.5 5.5 %fusion.18 = f32[1024,4,4]{2,1,0:T(4,128)S(1)} fusion(f32[1024,4,4]{2,1,0:T(4,128)} %gather_fusion, pred[1024]{0:T(1024)(128)(4,1)S(1)} %compare_and_fusion), kind=kLoop, calls=%fused_computation.49 | loop fusion | flops 16384 | bytes 132096
  67.0 3.0 %reshape.135 = f32[8,1,2048]{2,1,0:T(1,128)} reshape(f32[1024,4,4]{2,1,0:T(4,128)S(1)} %fusion.18) | data formatting | bytes 131072
  70.1 6.6 %all-to-all-start = ((f32[8,1,2048]{2,1,0:T(1,128)}), f32[8,1,2048]{2,1,0:T(1,128)S(1)}, u32[]{:S(2)}, u32[]{:S(2)}) async-start(f32[8,1,2048]{2,1,0:T(1,128)} %reshape.135), calls=%async_computation | async-start | bytes 131072 | tf_op jit(solution)/shard_map/all_to_all | solution.py:42
  76.6 0.0 all-gather.2.cloned.1.call-start
  76.6 0.0 copy-done.1
  76.6 0.0 copy-done.3
  76.7 0.1 fusion.17
  76.7 0.1 add_add_fusion
  76.8 4.8 %all-to-all-done = f32[8,1,2048]{2,1,0:T(1,128)S(1)} async-done(((f32[8,1,2048]{2,1,0:T(1,128)}), f32[8,1,2048]{2,1,0:T(1,128)S(1)}, u32[]{:S(2)}, u32[]{:S(2)}) %all-to-all-start) | async-done | bytes 65568 | tf_op jit(solution)/shard_map/all_to_all | solution.py:42
  81.6 0.5 broadcast.122
  82.1 0.8 reduce
  82.9 2.7 reshape.136
  85.6 0.8 copy.8
  86.5 0.1 add_divide_fusion
  86.6 0.1 multiply_convert_fusion
  86.7 0.1 constant_dynamic-update-slice_fusion
  86.8 0.0 copy-start
  86.8 0.8 copy-done
  87.6 0.0 all-gather.2.cloned.1.call-update
  87.7 64.6 %all-gather.2.cloned.1.call-done = bf16[2176,1024]{1,0:T(8,128)(2,1)} async-done(((bf16[2176,128]{1,0:T(8,128)(2,1)}), bf16[2176,1024]{1,0:T(8,128)(2,1)}) %all-gather.2.cloned.1.call-update) | async-done | bytes 4456464 | tf_op jit(solution)/shard_map/all_gather | solution.py:48
  152.2 4.9 %fusion.1 = f32[2176,272]{1,0:T(8,128)S(1)} fusion(bf16[2176,1024]{1,0:T(8,128)(2,1)} %all-gather.2.cloned.1.call-done, s32[]{:T(128)S(6)} %select_n.43), kind=kOutput, calls=%fused_computation.3 | convolution fusion | flops 1212153856 | bytes 7380996 | tf_op jit(solution)/shard_map/dot_general | solution.py:50
  157.1 0.0 copy-start.4
  157.2 75.4 %fusion = f32[80,272]{1,0:T(8,128)S(1)} fusion(f32[2176,272]{1,0:T(8,128)S(1)} %fusion.1), kind=kCustom, calls=%all-reduce-scatter | all-reduce-scatter fusion | flops 696321 | bytes 2455552
  232.6 4.4 %collective-permute-start.3 = (f32[80,272]{1,0:T(8,128)S(1)}, f32[80,272]{1,0:T(8,128)S(1)}, u32[]{:S(2)}, u32[]{:S(2)}) collective-permute-start(f32[80,272]{1,0:T(8,128)S(1)} %fusion), channel_id=1, source_target_pairs={{0,4},{1,5},{2,6},{3,7},{4,8},{5,9},{6,10},{7,11},{8,12},{9,13},{1... | collective-permute-start | bytes 261128
  236.9 8.4 %collective-permute-start.2 = (f32[80,272]{1,0:T(8,128)S(1)}, f32[80,272]{1,0:T(8,128)S(1)}, u32[]{:S(2)}, u32[]{:S(2)}) collective-permute-start(f32[80,272]{1,0:T(8,128)S(1)} %fusion), channel_id=1, source_target_pairs={{0,3},{1,4},{2,5},{3,6},{4,7},{5,8},{6,9},{7,10},{8,11},{9,12},{10... | collective-permute-start | bytes 261128
  245.3 10.9 %collective-permute-start.1 = (f32[80,272]{1,0:T(8,128)S(1)}, f32[80,272]{1,0:T(8,128)S(1)}, u32[]{:S(2)}, u32[]{:S(2)}) collective-permute-start(f32[80,272]{1,0:T(8,128)S(1)} %fusion), channel_id=1, source_target_pairs={{0,2},{1,3},{2,4},{3,5},{4,6},{5,7},{6,8},{7,9},{8,10},{9,11},{10,... | collective-permute-start | bytes 261128
  256.3 8.4 %collective-permute-start = (f32[80,272]{1,0:T(8,128)S(1)}, f32[80,272]{1,0:T(8,128)S(1)}, u32[]{:S(2)}, u32[]{:S(2)}) collective-permute-start(f32[80,272]{1,0:T(8,128)S(1)} %fusion), channel_id=1, source_target_pairs={{0,1},{1,2},{2,3},{3,4},{4,5},{5,6},{6,7},{7,8},{8,9},{9,10},{10,1... | collective-permute-start | bytes 261128
  264.7 1.9 collective-permute-start.4
  266.6 0.0 copy-done.4
  266.6 0.6 dynamic-slice.4
  267.9 4.8 %collective-permute-done.4 = f32[52,272]{1,0:T(8,128)S(1)} collective-permute-done((f32[52,272]{1,0:T(8,128)S(1)}, f32[52,272]{1,0:T(8,128)S(1)}, u32[]{:S(2)}, u32[]{:S(2)}) %collective-permute-start.4) | collective-permute-done | bytes 56608
  272.6 0.0 collective-permute-done.3
  272.6 0.0 collective-permute-done.2
  272.6 0.0 collective-permute-done.1
  272.7 0.0 collective-permute-done
  272.7 1.0 concatenate.50
  273.7 0.7 dynamic-slice_multiply_fusion
  (11 shorter events, 0.1 us)
Async XLA Ops:
  6.5 21.7 %copy-start.2 = (s32[1,128]{1,0:T(1,128)S(1)}, s32[1,128]{1,0:T(1,128)}, u32[]{:S(2)}) copy-start(s32[1,128]{1,0:T(1,128)} %param.5) | copy-start | bytes 1540
  28.2 48.4 %copy-start.1 = (f32[32]{0:T(128)S(1)}, f32[32]{0:T(128)}, u32[]{:S(2)}) copy-start(f32[32]{0:T(128)} %param.6) | copy-start | bytes 388
  28.2 48.4 %copy-start.3 = (s32[31]{0:T(128)S(1)}, s32[31]{0:T(128)}, u32[]{:S(2)}) copy-start(s32[31]{0:T(128)} %param.7) | copy-start | bytes 376
  70.1 11.5 %all-to-all-start = ((f32[8,1,2048]{2,1,0:T(1,128)}), f32[8,1,2048]{2,1,0:T(1,128)S(1)}, u32[]{:S(2)}, u32[]{:S(2)}) async-start(f32[8,1,2048]{2,1,0:T(1,128)} %reshape.135), calls=%async_computation | async-start | bytes 131072 | tf_op jit(solution)/shard_map/all_to_all | solution.py:42
  76.6 75.6 %all-gather.2.cloned.1.call-start = ((), (), s32[]{:S(2)}) async-start(), calls=%async_computation.1 | async-start | bytes 5013504 | tf_op jit(solution)/shard_map/all_gather | solution.py:48
  86.8 0.8 copy-start
  157.1 109.5 %copy-start.4 = (u32[256]{0:T(256)S(1)}, u32[256]{0:T(256)}, u32[]{:S(2)}) copy-start(u32[256]{0:T(256)} %constant.76) | copy-start | bytes 3076
  232.6 40.1 %collective-permute-start.3 = (f32[80,272]{1,0:T(8,128)S(1)}, f32[80,272]{1,0:T(8,128)S(1)}, u32[]{:S(2)}, u32[]{:S(2)}) collective-permute-start(f32[80,272]{1,0:T(8,128)S(1)} %fusion), channel_id=1, source_target_pairs={{0,4},{1,5},{2,6},{3,7},{4,8},{5,9},{6,10},{7,11},{8,12},{9,13},{1... | collective-permute-start | bytes 261128
  236.9 35.7 %collective-permute-start.2 = (f32[80,272]{1,0:T(8,128)S(1)}, f32[80,272]{1,0:T(8,128)S(1)}, u32[]{:S(2)}, u32[]{:S(2)}) collective-permute-start(f32[80,272]{1,0:T(8,128)S(1)} %fusion), channel_id=1, source_target_pairs={{0,3},{1,4},{2,5},{3,6},{4,7},{5,8},{6,9},{7,10},{8,11},{9,12},{10... | collective-permute-start | bytes 261128
  245.3 27.3 %collective-permute-start.1 = (f32[80,272]{1,0:T(8,128)S(1)}, f32[80,272]{1,0:T(8,128)S(1)}, u32[]{:S(2)}, u32[]{:S(2)}) collective-permute-start(f32[80,272]{1,0:T(8,128)S(1)} %fusion), channel_id=1, source_target_pairs={{0,2},{1,3},{2,4},{3,5},{4,6},{5,7},{6,8},{7,9},{8,10},{9,11},{10,... | collective-permute-start | bytes 261128
  256.3 16.4 %collective-permute-start = (f32[80,272]{1,0:T(8,128)S(1)}, f32[80,272]{1,0:T(8,128)S(1)}, u32[]{:S(2)}, u32[]{:S(2)}) collective-permute-start(f32[80,272]{1,0:T(8,128)S(1)} %fusion), channel_id=1, source_target_pairs={{0,1},{1,2},{2,3},{3,4},{4,5},{5,6},{6,7},{7,8},{8,9},{9,10},{10,1... | collective-permute-start | bytes 261128
  264.7 7.9 %collective-permute-start.4 = (f32[52,272]{1,0:T(8,128)S(1)}, f32[52,272]{1,0:T(8,128)S(1)}, u32[]{:S(2)}, u32[]{:S(2)}) collective-permute-start(f32[52,272]{1,0:T(8,128)S(1)} %slice.42), channel_id=1, source_target_pairs={{0,5},{1,6},{2,7},{3,8},{4,9},{5,10},{6,11},{7,12},{8,13},{9,14},{... | collective-permute-start | bytes 169736
Sparse Core Ops, SparseCore 0:
  87.8 64.4 all-gather.1
where the time goes:
time: 284 us; the launch traced here: 281 us
  blocking collectives  91.9 us (32%)
  waiting for transfers between devices  74.1 us (26%)
  local copies, waits for them, and re-layouts  48.2 us (17%)
  starting transfers between devices  40.6 us (14%)
  between operations  14.3 us (5%)
  other arithmetic  7.31 us (3%)
  matrix products  4.9 us (2%)
    unnamed x1, blocking collectives  75.4 us
    all_gather x1, waiting for transfers between devices, on_device(): block_features_bf = lax.all_gather(features_bf, 'lev', axis=1, tiled=True)  64.6 us
    unnamed x5, starting transfers between devices  34 us
    unnamed x20, local copies, waits for them, and re-layouts  30 us
    gather x1, local copies, waits for them, and re-layouts, on_device(): chosen = jnp.take(slab_fields, offsets, axis=2)  16.8 us
    all_gather x1, blocking collectives, on_device(): all_lists = lax.all_gather(sample_index, 'lev', axis=1, tiled=True)[0]  16.4 us
    all_to_all x1, starting transfers between devices, on_device(): lax.all_to_all(chosen, 'lev', split_axis=2, concat_axis=1, tiled=True)  6.56 us
  transfers between devices with their start and end apart: 7, of which 3 were waited for; matrix products, arithmetic and copies ran while one was open for 0% of the time, Pallas kernels for 0%

commit v1 on v0

--- a/solution.py
+++ b/solution.py
@@ -39,7 +39,10 @@
     group_cols = slab_fields.shape[2] // lev_count
     offsets = jnp.arange(all_lists.shape[0]) // samp_count * group_cols + all_lists
     chosen = jnp.take(slab_fields, offsets, axis=2)
-    picked_cols = lax.all_to_all(chosen, "lev", split_axis=2, concat_axis=1, tiled=True)
+    picked_cols = jnp.concatenate(
+        lax.all_to_all(jnp.stack(jnp.split(chosen, lax.axis_size("lev"), axis=2)), "lev", 0, 0),
+        axis=1,
+    )
     smooth = vertical_filter(picked_cols, thickness, level_cuts)
     feat_count = 4 * smooth.shape[1] + 2 * smooth.shape[1] * smooth.shape[1]
     col_count = feat_count // lev_count

time: 284 us -> 274 us (0.965)
  the two profiles are of different devices: /device:TPU:26 before, /device:TPU:171 now
where the time goes in v1:
time: 274 us; the launch traced here: 271 us
  waiting for transfers between devices  90.9 us (33%)
  blocking collectives  90.8 us (33%)
  local copies, waits for them, and re-layouts  37.7 us (14%)
  starting transfers between devices  27.9 us (10%)
  between operations  14.3 us (5%)
  matrix products  4.9 us (2%)
  other arithmetic  4.77 us (2%)
    unnamed x1, blocking collectives  78.9 us
    all_gather x1, waiting for transfers between devices, on_device(): block_features_bf = lax.all_gather(features_bf, 'lev', axis=1, tiled=True)  66.4 us
    unnamed x23, local copies, waits for them, and re-layouts  24.4 us
    unnamed x6, waiting for transfers between devices  21.4 us
    unnamed x5, starting transfers between devices  21.2 us
    all_gather x1, blocking collectives, on_device(): all_lists = lax.all_gather(sample_index, 'lev', axis=1, tiled=True)[0]  11.9 us
    gather x1, local copies, waits for them, and re-layouts, on_device(): chosen = jnp.take(slab_fields, offsets, axis=2)  11.7 us
    all_to_all x1, starting transfers between devices, on_device(): lax.all_to_all(jnp.stack(jnp.split(chosen, lax.axis_size('lev'), axis=2))...  6.69 us
  transfers between devices with their start and end apart: 7, of which 3 were waited for; matrix products, arithmetic and copies ran while one was open for 0% of the time, Pallas kernels for 0%

profile of v1, /device:TPU:171, one launch (start us, length us, event | category | flops | bytes accessed | tf_op | source)
XLA Modules:
  0.0 271.3 jit_solution(6795734570368282034)
XLA Ops:
  6.5 11.9 %all_gather.6 = s32[1,1024]{1,0:T(1,128)S(1)} all-gather(s32[1,128]{1,0:T(1,128)} %param.5), channel_id=1, replica_groups=mesh['lev'=8,'hor'=32] {'lev'}, dimensions={1}, use_global_device_ids=true | all-gather | bytes 4608 | tf_op jit(solution)/shard_map/all_gather | solution.py:38
  18.4 21.7 %copy.18 = f32[4,4,16384]{1,0,2:T(4,128)} copy(f32[4,4,16384]{2,1,0:T(4,128)} %param.4) | data formatting | bytes 2097152 | tf_op args[0]
  40.1 11.7 %gather_fusion = f32[1024,4,4]{2,1,0:T(4,128)S(1)} fusion(f32[4,4,16384]{1,0,2:T(4,128)} %copy.18, s32[1024]{0:T(1024)S(1)} %broadcast_clamp_fusion), kind=kCustom, calls=%fused_computation | custom fusion | bytes 135168 | tf_op jit(solution)/shard_map/jit(_take)/gather | solution.py:41
  51.9 3.7 %select_bitcast_fusion = f32[4,4,1024]{1,0,2:T(4,128)S(1)} fusion(f32[1024,4,4]{2,1,0:T(4,128)S(1)} %gather_fusion, pred[1024]{0:T(1024)(128)(4,1)S(1)} %compare_and_fusion), kind=kLoop, calls=%fused_computation.1 | loop fusion | flops 16384 | bytes 132096 | tf_op jit(solution)/shard_map/jit(_take)/select_n | solution.py:41
  55.8 0.0 copy-start.1
  55.8 0.0 copy-start.2
  56.0 1.4 copy.19
  57.4 6.7 %all-to-all-start = ((f32[8,4,4,128]{3,2,1,0:T(4,128)}), f32[8,4,4,128]{3,2,1,0:T(4,128)S(1)}, u32[]{:S(2)}, u32[]{:S(2)}) async-start(f32[8,4,4,128]{3,2,1,0:T(4,128)} %copy.19), calls=%async_computation | async-start | bytes 131072 | tf_op jit(solution)/shard_map/all_to_all | solution.py:43
  64.1 0.0 all-gather.2.cloned.1.call-start
  64.1 0.0 copy-done.1
  64.1 0.0 copy-done.2
  64.1 0.1 fusion.25
  64.2 0.1 add_add_fusion
  64.3 3.1 %all-to-all-done = f32[8,4,4,128]{3,2,1,0:T(4,128)S(1)} async-done(((f32[8,4,4,128]{3,2,1,0:T(4,128)}), f32[8,4,4,128]{3,2,1,0:T(4,128)S(1)}, u32[]{:S(2)}, u32[]{:S(2)}) %all-to-all-start) | async-done | bytes 65568 | tf_op jit(solution)/shard_map/all_to_all | solution.py:43
  67.4 0.1 add_divide_fusion
  67.6 0.1 multiply_convert_fusion
  67.7 0.1 constant_dynamic-update-slice_fusion
  67.8 0.0 copy-start
  67.8 0.8 copy-done
  68.6 0.0 all-gather.2.cloned.1.call-update
  68.6 66.4 %all-gather.2.cloned.1.call-done = bf16[2176,1024]{1,0:T(8,128)(2,1)} async-done(((bf16[2176,128]{1,0:T(8,128)(2,1)}), bf16[2176,1024]{1,0:T(8,128)(2,1)}) %all-gather.2.cloned.1.call-update) | async-done | bytes 4456464 | tf_op jit(solution)/shard_map/all_gather | solution.py:51
  135.0 4.9 %fusion.1 = f32[2176,272]{1,0:T(8,128)S(1)} fusion(bf16[2176,1024]{1,0:T(8,128)(2,1)} %all-gather.2.cloned.1.call-done, s32[]{:T(128)S(6)} %select_n.43), kind=kOutput, calls=%fused_computation.3 | convolution fusion | flops 1212153856 | bytes 7380996 | tf_op jit(solution)/shard_map/dot_general | solution.py:53
  139.9 0.0 copy-start.3
  140.0 78.9 %fusion = f32[80,272]{1,0:T(8,128)S(1)} fusion(f32[2176,272]{1,0:T(8,128)S(1)} %fusion.1), kind=kCustom, calls=%all-reduce-scatter | all-reduce-scatter fusion | flops 696321 | bytes 2455552
  218.9 3.7 %collective-permute-start = (f32[80,272]{1,0:T(8,128)S(1)}, f32[80,272]{1,0:T(8,128)S(1)}, u32[]{:S(2)}, u32[]{:S(2)}) collective-permute-start(f32[80,272]{1,0:T(8,128)S(1)} %fusion), channel_id=1, source_target_pairs={{0,1},{1,2},{2,3},{3,4},{4,5},{5,6},{6,7},{7,8},{8,9},{9,10},{10,1... | collective-permute-start | bytes 261128
  222.6 2.0 collective-permute-start.1
  224.5 9.5 %collective-permute-start.2 = (f32[80,272]{1,0:T(8,128)S(1)}, f32[80,272]{1,0:T(8,128)S(1)}, u32[]{:S(2)}, u32[]{:S(2)}) collective-permute-start(f32[80,272]{1,0:T(8,128)S(1)} %fusion), channel_id=1, source_target_pairs={{0,3},{1,4},{2,5},{3,6},{4,7},{5,8},{6,9},{7,10},{8,11},{9,12},{10... | collective-permute-start | bytes 261128
  234.0 1.9 collective-permute-start.3
  236.0 4.2 %collective-permute-start.4 = (f32[52,272]{1,0:T(8,128)S(1)}, f32[52,272]{1,0:T(8,128)S(1)}, u32[]{:S(2)}, u32[]{:S(2)}) collective-permute-start(f32[52,272]{1,0:T(8,128)S(1)} %slice.42), channel_id=1, source_target_pairs={{0,5},{1,6},{2,7},{3,8},{4,9},{5,10},{6,11},{7,12},{8,13},{9,14},{... | collective-permute-start | bytes 169736
  240.1 0.0 copy-done.3
  240.1 0.6 dynamic-slice.4
  241.4 21.4 %collective-permute-done.4 = f32[52,272]{1,0:T(8,128)S(1)} collective-permute-done((f32[52,272]{1,0:T(8,128)S(1)}, f32[52,272]{1,0:T(8,128)S(1)}, u32[]{:S(2)}, u32[]{:S(2)}) %collective-permute-start.4) | collective-permute-done | bytes 56608
  262.8 0.0 collective-permute-done
  262.8 0.0 collective-permute-done.1
  262.8 0.0 collective-permute-done.2
  262.8 0.0 collective-permute-done.3
  262.8 1.0 concatenate.50
  263.8 0.7 dynamic-slice_multiply_fusion
  (20 shorter events, 0.4 us)
Async XLA Ops:
  55.8 8.3 %copy-start.1 = (f32[32]{0:T(128)S(1)}, f32[32]{0:T(128)}, u32[]{:S(2)}) copy-start(f32[32]{0:T(128)} %param.6) | copy-start | bytes 388
  55.8 8.3 %copy-start.2 = (s32[31]{0:T(128)S(1)}, s32[31]{0:T(128)}, u32[]{:S(2)}) copy-start(s32[31]{0:T(128)} %param.7) | copy-start | bytes 376
  57.4 10.0 %all-to-all-start = ((f32[8,4,4,128]{3,2,1,0:T(4,128)}), f32[8,4,4,128]{3,2,1,0:T(4,128)S(1)}, u32[]{:S(2)}, u32[]{:S(2)}) async-start(f32[8,4,4,128]{3,2,1,0:T(4,128)} %copy.19), calls=%async_computation | async-start | bytes 131072 | tf_op jit(solution)/shard_map/all_to_all | solution.py:43
  64.1 70.9 %all-gather.2.cloned.1.call-start = ((), (), s32[]{:S(2)}) async-start(), calls=%async_computation.1 | async-start | bytes 5013504 | tf_op jit(solution)/shard_map/all_gather | solution.py:51
  67.8 0.8 copy-start
  139.9 100.2 %copy-start.3 = (u32[256]{0:T(256)S(1)}, u32[256]{0:T(256)}, u32[]{:S(2)}) copy-start(u32[256]{0:T(256)} %constant.76) | copy-start | bytes 3076
  218.9 43.8 %collective-permute-start = (f32[80,272]{1,0:T(8,128)S(1)}, f32[80,272]{1,0:T(8,128)S(1)}, u32[]{:S(2)}, u32[]{:S(2)}) collective-permute-start(f32[80,272]{1,0:T(8,128)S(1)} %fusion), channel_id=1, source_target_pairs={{0,1},{1,2},{2,3},{3,4},{4,5},{5,6},{6,7},{7,8},{8,9},{9,10},{10,1... | collective-permute-start | bytes 261128
  222.6 40.2 %collective-permute-start.1 = (f32[80,272]{1,0:T(8,128)S(1)}, f32[80,272]{1,0:T(8,128)S(1)}, u32[]{:S(2)}, u32[]{:S(2)}) collective-permute-start(f32[80,272]{1,0:T(8,128)S(1)} %fusion), channel_id=1, source_target_pairs={{0,2},{1,3},{2,4},{3,5},{4,6},{5,7},{6,8},{7,9},{8,10},{9,11},{10,... | collective-permute-start | bytes 261128
  224.5 38.2 %collective-permute-start.2 = (f32[80,272]{1,0:T(8,128)S(1)}, f32[80,272]{1,0:T(8,128)S(1)}, u32[]{:S(2)}, u32[]{:S(2)}) collective-permute-start(f32[80,272]{1,0:T(8,128)S(1)} %fusion), channel_id=1, source_target_pairs={{0,3},{1,4},{2,5},{3,6},{4,7},{5,8},{6,9},{7,10},{8,11},{9,12},{10... | collective-permute-start | bytes 261128
  234.0 28.7 %collective-permute-start.3 = (f32[80,272]{1,0:T(8,128)S(1)}, f32[80,272]{1,0:T(8,128)S(1)}, u32[]{:S(2)}, u32[]{:S(2)}) collective-permute-start(f32[80,272]{1,0:T(8,128)S(1)} %fusion), channel_id=1, source_target_pairs={{0,4},{1,5},{2,6},{3,7},{4,8},{5,9},{6,10},{7,11},{8,12},{9,13},{1... | collective-permute-start | bytes 261128
  236.0 26.8 %collective-permute-start.4 = (f32[52,272]{1,0:T(8,128)S(1)}, f32[52,272]{1,0:T(8,128)S(1)}, u32[]{:S(2)}, u32[]{:S(2)}) collective-permute-start(f32[52,272]{1,0:T(8,128)S(1)} %slice.42), channel_id=1, source_target_pairs={{0,5},{1,6},{2,7},{3,8},{4,9},{5,10},{6,11},{7,12},{8,13},{9,14},{... | collective-permute-start | bytes 169736
Sparse Core Ops, SparseCore 0:
  68.7 66.2 all-gather.1
